TPU v7x, 32 devices: a whole 2x2x4 slice. The times are simulated.
32 devices in a mesh: row: 8 (over y, x, core), section: 4 (over z).
Axes of the slice: x: 2, y: 2, z: 4, core: 2. Of those that a mesh axis runs over, the one named last changes fastest.
Arguments:
- features: bfloat16 [8192, 256], P('row'), may hold values from -6 to 6
- weight: bfloat16 [256, 256], replicated, may hold values from -0.375 to 0.375
- cotangent: bfloat16 [8192, 256], P('row'), may hold values from -0.0625 to 0.0625
- counts: int32 [64, 16, 128, 128], P('row', 'section'), may hold values from 0 to 3, as said below
- columns: int32 [64, 16], P('row', 'section'), may hold values from 0 to 63, as said below
- live_slots: int32 [64, 4], P('row', 'section'), may hold values from 1 to 4, as said below
Outputs:
- output: bfloat16 [8192, 256], P('row')
- grad_weight: float32 [256, 256], replicated
Inputs may be any that keep to these rules, and one draw needn't show every extreme that they name: `columns`: every entry in a slot of section index s names a node block g with (g // 8) % 4 == s; the 4 slots of one row of blocks and one section index name distinct column blocks. Slots at k >= live_slots[b, s] are ignored; the value 4 occurs at every section index in every draw. `counts`: most entries are zero.
All inputs are finite; a program needn't handle non-finite values.
Results may differ from a plain program's by a relative error of at most 0.0055.
Values may be sent and summed in bfloat16 or wider, within the bound.
A program may use at most 64 MiB of HBM per device.

v0:
```python
import jax
import jax.numpy as jnp
from jax import lax
from jax.sharding import PartitionSpec as P


def per_device(features, weight, cotangent, counts, columns, live_slots):
    row_count = features.shape[0]
    feat_width = features.shape[1]
    block_count = columns.shape[0]
    slot_count = columns.shape[1]
    block_size = counts.shape[2]
    section_index = lax.axis_index("section")
    section_count = lax.axis_size("section")
    owner_count = lax.axis_size("row") // section_count
    everything = lax.all_gather(features, "row", axis=0, tiled=True)
    grouped = everything.reshape(owner_count, section_count, row_count, feat_width)
    window = lax.dynamic_index_in_dim(grouped, section_index, 1, keepdims=False)
    window = window.reshape(owner_count * block_count, block_size, feat_width)
    local_cols = columns // block_count // section_count * block_count + columns % block_count
    slot_used = jnp.arange(slot_count, dtype=jnp.int32)[None, :] < live_slots
    masked = jnp.where(slot_used[:, :, None, None], counts, 0)
    degree = jnp.sum(masked, axis=(1, 3)).astype(jnp.float32).reshape(row_count)
    edge_mats = masked.astype(jnp.bfloat16)
    picked = window[local_cols]
    partial_value = jnp.einsum(
        "rkij,rkjf->rif", edge_mats, picked, preferred_element_type=jnp.float32
    )
    partial_value = partial_value.reshape(row_count, feat_width)
    summed, degree_all = lax.psum((partial_value, degree), "section")
    aggregate = (summed * lax.rsqrt(1.0 + degree_all)[:, None]).astype(jnp.bfloat16)
    pre_act = jnp.dot(aggregate, weight, preferred_element_type=jnp.float32)
    gate_value = jax.nn.sigmoid(pre_act)
    output = (pre_act * gate_value).astype(jnp.bfloat16)
    grad_pre = (
        cotangent.astype(jnp.float32) * gate_value * (1.0 + pre_act * (1.0 - gate_value))
    ).astype(jnp.bfloat16)
    grad_local = lax.dot_general(
        aggregate, grad_pre, (((0,), (0,)), ((), ())), preferred_element_type=jnp.float32
    )
    grad_weight = lax.psum(grad_local, "row")
    return (output, grad_weight)


def solution(mesh):
    in_specs = (
        P("row", None),
        P(),
        P("row", None),
        P("row", "section", None, None),
        P("row", "section"),
        P("row", "section"),
    )
    out_specs = (P("row", None), P())
    return jax.shard_map(
        per_device, mesh=mesh, in_specs=in_specs, out_specs=out_specs, check_vma=False
    )
```

profile of v0, /device:TPU:0, one launch (start us, length us, event | category | flops | bytes accessed | tf_op | source)
XLA Modules:
  0.0 172.0 jit_solution(4953633193396426414)
XLA Ops:
  7.2 0.0 copy-start
  7.2 0.0 all-gather.2.cloned.1.call-start
  7.2 0.7 all-gather.2.cloned.1.call-update
  7.9 0.0 all-reduce.3.cloned.1.call-start
  8.0 0.7 compare_select_fusion
  8.7 0.1 copy.9
  8.8 0.1 reshape.45
  8.8 0.7 iota_compare_fusion
  9.6 39.8 %all-gather.2.cloned.1.call-done = bf16[8192,256]{1,0:T(8,128)(2,1)} async-done(((bf16[1024,256]{1,0:T(8,128)(2,1)}), bf16[8192,256]{1,0:T(8,128)(2,1)}) %all-gather.2.cloned.1.call-update) | async-done | bytes 4194320 | tf_op jit(solution)/shard_map/all_gather | solution.py:16
  49.4 1.3 constant_dynamic-slice_fusion
  50.6 0.7 gather_fusion
  51.3 3.2 %fusion = f32[8,128,256,1]{2,1,3,0:T(8,128)} fusion(bf16[8,4,128,256]{3,2,1,0:T(8,128)(2,1)S(1)} %bitcast.13, s32[8,4,128,128]{3,2,1,0:T(8,128)} %param.9, pred[8,4]{1,0:T(8,128)(4,1)S(1)} %iota_compare_fusion), kind=kOutput, calls=%fused_computation.3 | convolution fusion | flops 269484032 | bytes 5242912 | tf_op jit(solution)/shard_map/rkij,rkjf->rif/dot_general | solution.py:26
  54.5 0.0 all-reduce.3.cloned.1.call-update
  54.5 0.0 all-reduce.5.cloned.1.call-start
  54.6 1.9 %select_reduce_fusion = s32[8,128]{1,0:T(8,128)S(1)} fusion(s32[8,4,128,128]{3,2,1,0:T(8,128)} %param.9, pred[8,4]{1,0:T(8,128)(4,1)S(1)} %iota_compare_fusion), kind=kLoop, calls=%fused_computation.1 | loop fusion | flops 1047552 | bytes 2101280 | tf_op jit(solution)/shard_map/reduce_sum | solution.py:23
  56.5 11.9 %psum.22 = f32[1024]{0:T(1024)S(1)} all-reduce(f32[1024]{0:T(1024)S(1)} %convert_bitcast_fusion), channel_id=1, replica_groups=mesh['row'=8,'section'=4] {'section'}, use_global_device_ids=true, to_apply=%region_2.3 | all-reduce | flops 1024 | bytes 8192 | tf_op jit(solution)/shard_map/psum | solution.py:30
  68.5 0.0 copy-start.2
  68.5 38.2 %all-reduce.3.cloned.1.call-done = f32[1024,256]{1,0:T(8,128)} async-done(((f32[1024,256]{1,0:T(8,128)}), f32[1024,256]{1,0:T(8,128)}) %all-reduce.3.cloned.1.call-update) | async-done | bytes 1048592 | tf_op jit(solution)/shard_map/psum | solution.py:30
  106.6 0.0 copy-done
  106.6 0.0 copy-start.1
  106.6 2.6 %multiply_convert_fusion.1 = (bf16[1024,256]{1,0:T(8,128)(2,1)}, f32[1024,256]{1,0:T(8,128)S(1)}) fusion(bf16[256,256]{1,0:T(8,128)(2,1)S(1)} %copy-done, f32[1024,256]{1,0:T(8,128)} %all-reduce.3.cloned.1.call-done, f32[1024]{0:T(1024)S(1)} %add_rsqrt_fusion), kind=kOutput, calls=%fused_computation.5 | convolution fusion | flops 136052736 | bytes 2756608 | tf_op jit(solution)/shard_map/dot_general | solution.py:32
  109.2 0.0 copy-done.2
  109.2 0.0 copy-done.1
  109.2 1.5 fusion.3
  110.7 0.0 all-reduce.5.cloned.1.call-update
  110.7 53.1 %all-reduce.5.cloned.1.call-done = f32[256,256]{1,0:T(8,128)} async-done(((f32[256,256]{1,0:T(8,128)}), f32[256,256]{1,0:T(8,128)}) %all-reduce.5.cloned.1.call-update) | async-done | bytes 262160 | tf_op jit(solution)/shard_map/psum | solution.py:41
  163.8 1.7 copy.13
  (3 shorter events, 0.0 us)
Async XLA Ops:
  7.2 99.5 %copy-start = (bf16[256,256]{1,0:T(8,128)(2,1)S(1)}, bf16[256,256]{1,0:T(8,128)(2,1)}, u32[]{:S(2)}) copy-start(bf16[256,256]{1,0:T(8,128)(2,1)} %param.7) | copy-start | bytes 393220
  7.2 42.2 %all-gather.2.cloned.1.call-start = ((), (), s32[]{:S(2)}) async-start(), calls=%async_computation | async-start | bytes 4718592 | tf_op jit(solution)/shard_map/all_gather | solution.py:16
  7.9 98.7 %all-reduce.3.cloned.1.call-start = ((), (), s32[]{:S(2)}) async-start(), calls=%async_computation.1 | async-start | bytes 2097152 | tf_op jit(solution)/shard_map/psum | solution.py:30
  54.5 109.3 %all-reduce.5.cloned.1.call-start = ((), (), s32[]{:S(2)}) async-start(), calls=%async_computation.2 | async-start | bytes 524288 | tf_op jit(solution)/shard_map/psum | solution.py:41
  68.5 40.8 %copy-start.2 = (bf16[1024,256]{1,0:T(8,128)(2,1)S(1)}, bf16[1024,256]{1,0:T(8,128)(2,1)}, u32[]{:S(2)}) copy-start(bf16[1024,256]{1,0:T(8,128)(2,1)} %param.8) | copy-start | bytes 1572868
  106.6 2.6 %copy-start.1 = (f32[1024,256]{1,0:T(8,128)S(1)}, f32[1024,256]{1,0:T(8,128)}, u32[]{:S(2)}) copy-start(f32[1024,256]{1,0:T(8,128)} %all-reduce.3.cloned.1.call-done) | copy-start | bytes 3145732
Sparse Core Ops, SparseCore 0:
  9.9 39.4 all-gather.1
  54.7 51.9 all-reduce.2
  110.8 52.9 all-reduce.4
where the time goes:
time: 172 us
  waiting for transfers between devices  132 us (77%)
  between operations  13.8 us (8%)
  blocking collectives  11.9 us (7%)
  matrix products  7.25 us (4%)
  local copies, waits for them, and re-layouts  3.82 us (2%)
  other arithmetic  3.35 us (2%)
    psum x1, waiting for transfers between devices, per_device(): grad_weight = lax.psum(grad_local, 'row')  53.1 us
    all_gather x1, waiting for transfers between devices, per_device(): everything = lax.all_gather(features, 'row', axis=0, tiled=True)  39.8 us
    psum x1, waiting for transfers between devices, per_device(): summed, degree_all = lax.psum((partial_value, degree), 'section')  38.2 us
    psum x1, blocking collectives, per_device(): summed, degree_all = lax.psum((partial_value, degree), 'section')  11.9 us
  transfers between devices with their start and end apart: 3, of which 3 were waited for; matrix products, arithmetic and copies ran while one was open for 2% of the time, Pallas kernels for 0%

commit v1 on v0

v1 whole, which is shorter than its diff:
```python
import functools

import jax
import jax.numpy as jnp
from jax import lax
from jax.experimental import pallas as pl
from jax.experimental.pallas import tpu as pltpu
from jax.sharding import PartitionSpec as P

MESH = pl.DeviceIdType.MESH


def remote(src, dst, send_sem, recv_sem, where):
    return pltpu.make_async_remote_copy(
        src_ref=src, dst_ref=dst, send_sem=send_sem, recv_sem=recv_sem,
        device_id=where, device_id_type=MESH,
    )


def kernel(
    rows, sections, plane,
    live, cols, feat, weight, cot, counts,
    out, gw_out,
    cnt_v, cot_v, w_v, edge, win, deg_all, scale, part32, part16, rs_in,
    gw32, g_send, ga_in, gb_in,
    l_sem, f_ssem, f_rsem, d_ssem, d_rsem, rs_ssem, rs_rsem, o_ssem, o_rsem,
    ga_ssem, ga_rsem, gb_ssem, gb_rsem, gc_ssem, gc_rsem,
):
    row = lax.axis_index("row")
    sec = lax.axis_index("section")
    blocks, slots, size, _ = cnt_v.shape
    width = win.shape[-1]
    turns = rows // sections
    span = rs_in.shape[1]
    grain = gw_out.shape[1]

    loads = [
        pltpu.make_async_copy(counts, cnt_v, l_sem.at[0]),
        pltpu.make_async_copy(weight, w_v, l_sem.at[1]),
        pltpu.make_async_copy(cot.at[sec], cot_v, l_sem.at[2]),
    ]
    for load in loads:
        load.start()

    barrier = pltpu.get_barrier_semaphore()
    for j in range(1, rows):
        pl.semaphore_signal(barrier, inc=1, device_id={"row": lax.rem(row + j, rows)}, device_id_type=MESH)
    for j in range(1, sections):
        pl.semaphore_signal(barrier, inc=1, device_id={"section": lax.rem(sec + j, sections)}, device_id_type=MESH)
    pl.semaphore_wait(barrier, rows - 1 + sections - 1)

    own = [row == t * sections + sec for t in range(turns)]
    keep = [pltpu.make_async_copy(feat, win.at[pl.ds(t * blocks, blocks)], l_sem.at[3]) for t in range(turns)]
    sends = []
    if plane:
        half = blocks // 2
        y, x, c = row // 4, lax.rem(row // 2, 2), lax.rem(row, 2)
        home_x = sec // 2
        sib = row + 1 - 2 * c

        def chunk(t, i, kind, where):
            return remote(
                win.at[t * blocks + i], win.at[t * blocks + i],
                f_ssem.at[kind, t, i], f_rsem.at[t, i], {"row": where},
            )

        for t in range(turns):
            def first(t=t, act="start"):
                for k in range(half):
                    for h in range(2):
                        i = h * half + k
                        for kind, where in (
                            (0, (1 - y) * 4 + x * 2 + h),
                            (1, y * 4 + (1 - x) * 2 + h),
                            (2, sib),
                        ):
                            d = remote(
                                feat.at[i], win.at[t * blocks + i],
                                f_ssem.at[kind, t, i], f_rsem.at[t, i], {"row": where},
                            )
                            if act == "start":
                                d.start()
                            else:
                                d.wait_send()

            @pl.when(own[t])
            def _(first=first, t=t):
                keep[t].start()
                first()

            sends.append((own[t], functools.partial(first, act="wait")))
    else:
        for t in range(turns):
            def direct(j, t):
                return remote(
                    feat, win.at[pl.ds(t * blocks, blocks)],
                    f_ssem.at[t, j], f_rsem.at[t, 0], {"row": lax.rem(row + j, rows)},
                )

            def first(act, t=t, direct=direct):
                def body(j, carry):
                    d = direct(j, t)
                    if act == "start":
                        d.start()
                    else:
                        d.wait_send()
                    return carry
                lax.fori_loop(1, rows, body, 0)

            @pl.when(own[t])
            def _(first=first, t=t):
                keep[t].start()
                first("start")

            sends.append((own[t], functools.partial(first, "wait")))

    loads[0].wait()
    ones = jnp.ones((8, size), jnp.bfloat16)

    def prepare(b, carry):
        total = jnp.zeros((size, size), jnp.int32)
        for k in range(slots):
            e = jnp.where(k < live[b, 0], cnt_v[b, k], 0)
            total = total + e
            edge[b, :, k * size:(k + 1) * size] = e.astype(jnp.float32).astype(jnp.bfloat16)
        d = lax.dot_general(
            ones, total.astype(jnp.float32).astype(jnp.bfloat16), (((1,), (1,)), ((), ())),
            preferred_element_type=jnp.float32,
        )
        deg_all[sec, pl.ds(b, 1), :] = d[0:1]
        return carry

    lax.fori_loop(0, blocks, prepare, 0)
    deg_copies = []
    for j in range(1, sections):
        peer = lax.rem(sec + j, sections)
        d = remote(deg_all.at[sec], deg_all.at[sec], d_ssem.at[j], d_rsem.at[sec], {"section": peer})
        d.start()
        deg_copies.append(d)

    if plane:
        off_chip = [jnp.logical_not((y == t) & (x == home_x)) for t in range(turns)]
        pass_on = [(y == t) & (x != home_x) for t in range(turns)]
        across = (1 - y) * 4 + x * 2 + c
        for k in range(half):
            for t in range(turns):
                i = c * half + k

                @pl.when(off_chip[t])
                def _(i=i, t=t):
                    chunk(t, i, 2, sib).wait_recv()
                    chunk(t, i, 2, sib).start()

                    @pl.when(pass_on[t])
                    def _():
                        chunk(t, i, 0, across).start()
        for t in range(turns):
            def other(t=t):
                for k in range(half):
                    chunk(t, (1 - c) * half + k, 2, sib).wait_recv()

            def mine(t=t):
                for k in range(half):
                    chunk(t, c * half + k, 2, sib).wait_recv()

            @pl.when(jnp.logical_not(own[t]))
            def _(other=other):
                other()

            @pl.when((y == t) & (x == home_x) & jnp.logical_not(own[t]))
            def _(mine=mine):
                mine()

            @pl.when(own[t])
            def _(t=t):
                keep[t].wait()

            def relayed(t=t):
                for k in range(half):
                    chunk(t, c * half + k, 2, sib).wait_send()

            def crossed(t=t):
                for k in range(half):
                    chunk(t, c * half + k, 0, across).wait_send()

            sends.append((off_chip[t], relayed))
            sends.append((pass_on[t], crossed))
    else:
        for t in range(turns):
            @pl.when(own[t])
            def _(t=t):
                keep[t].wait()

            @pl.when(jnp.logical_not(own[t]))
            def _(t=t):
                direct(1, t).wait_recv()

    def block_sum(b):
        acc = jnp.zeros((size, width), jnp.float32)
        for k in range(0, slots, 2):
            picked = []
            for q in (k, k + 1):
                g = cols[b, q]
                picked.append(win[lax.div(lax.div(g, blocks), sections) * blocks + lax.rem(g, blocks)])
            acc = acc + jnp.dot(
                edge[b, :, k * size:(k + 2) * size], jnp.concatenate(picked, axis=0),
                preferred_element_type=jnp.float32,
            )
        at = pl.ds(pl.multiple_of(b * size, size), size)
        part32[at, :] = acc
        part16[at, :] = acc.astype(jnp.bfloat16)

    per = span // size
    if per == 0:
        for b in range(blocks):
            block_sum(b)
    rs_copies = []
    for j in range(1, sections + 1):
        peer = lax.rem(sec + j, sections)
        for q in range(per):
            block_sum(peer * per + q)
        if j < sections:
            d = remote(
                part16.at[pl.ds(pl.multiple_of(peer * span, span), span)], rs_in.at[sec],
                rs_ssem.at[j], rs_rsem.at[sec], {"section": peer},
            )
            d.start()
            rs_copies.append(d)

    for j in range(1, sections):
        peer = lax.rem(sec + j, sections)
        remote(deg_all.at[peer], deg_all.at[peer], d_ssem.at[j], d_rsem.at[peer], {"section": peer}).wait_recv()
    degree = deg_all[0]
    for z in range(1, sections):
        degree = degree + deg_all[z]
    inv = lax.rsqrt(1.0 + degree).T
    for b in range(blocks):
        scale[b * size:(b + 1) * size, :] = jnp.broadcast_to(inv[:, b:b + 1], (size, size))

    mine_at = pl.ds(pl.multiple_of(sec * span, span), span)
    total = part32[mine_at, :]
    for j in range(1, sections):
        peer = lax.rem(sec + j, sections)
        remote(rs_in.at[peer], rs_in.at[peer], rs_ssem.at[j], rs_rsem.at[peer], {"section": peer}).wait_recv()
        total = total + rs_in[peer].astype(jnp.float32)
    own_scale = scale[mine_at, :]
    aggregate = (total * jnp.concatenate([own_scale] * (width // size), axis=1)).astype(jnp.bfloat16)

    loads[1].wait()
    loads[2].wait()
    pre = jnp.dot(aggregate, w_v[...], preferred_element_type=jnp.float32)
    gate = jax.nn.sigmoid(pre)
    out[sec] = (pre * gate).astype(jnp.bfloat16)
    grad_pre = (cot_v[...].astype(jnp.float32) * gate * (1.0 + pre * (1.0 - gate))).astype(jnp.bfloat16)
    grad = lax.dot_general(aggregate, grad_pre, (((0,), (0,)), ((), ())), preferred_element_type=jnp.float32)
    grad = grad.reshape(rows, grain, width)
    gw32[...] = grad
    g_send[...] = grad.astype(jnp.bfloat16)

    tail = []
    for j in range(1, rows):
        peer = lax.rem(row + j, rows)
        d = remote(g_send.at[peer], ga_in.at[row], ga_ssem.at[j], ga_rsem.at[row], {"row": peer})
        d.start()
        tail.append(d)
    out_copies = []
    for j in range(1, sections):
        peer = lax.rem(sec + j, sections)
        d = remote(out.at[sec], out.at[sec], o_ssem.at[j], o_rsem.at[sec], {"section": peer})
        d.start()
        out_copies.append(d)

    acc = gw32[row]
    for j in range(1, rows):
        peer = lax.rem(row + j, rows)
        remote(ga_in.at[peer], ga_in.at[peer], ga_ssem.at[j], ga_rsem.at[peer], {"row": peer}).wait_recv()
        acc = acc + ga_in[peer].astype(jnp.float32)
    gb_in[sec] = acc
    for j in range(1, sections):
        peer = lax.rem(sec + j, sections)
        d = remote(gb_in.at[sec], gb_in.at[sec], gb_ssem.at[j], gb_rsem.at[sec], {"section": peer})
        d.start()
        tail.append(d)
    for j in range(1, sections):
        peer = lax.rem(sec + j, sections)
        remote(gb_in.at[peer], gb_in.at[peer], gb_ssem.at[j], gb_rsem.at[peer], {"section": peer}).wait_recv()
    acc = gb_in[0]
    for z in range(1, sections):
        acc = acc + gb_in[z]
    gw_out[row] = acc
    for j in range(1, rows):
        peer = lax.rem(row + j, rows)
        d = remote(gw_out.at[row], gw_out.at[row], gc_ssem.at[j], gc_rsem.at[row], {"row": peer})
        d.start()
        tail.append(d)
    for j in range(1, rows):
        peer = lax.rem(row + j, rows)
        remote(gw_out.at[peer], gw_out.at[peer], gc_ssem.at[j], gc_rsem.at[peer], {"row": peer}).wait_recv()
    for j in range(1, sections):
        peer = lax.rem(sec + j, sections)
        remote(out.at[peer], out.at[peer], o_ssem.at[j], o_rsem.at[peer], {"section": peer}).wait_recv()

    for cond, finish in sends:
        pl.when(cond)(finish)
    for d in deg_copies + rs_copies + out_copies + tail:
        d.wait_send()


def per_device(rows, sections, plane, features, weight, cotangent, counts, columns, live_slots):
    count, width = features.shape
    blocks, slots, size, _ = counts.shape
    span = count // sections
    grain = width // rows
    turns = rows // sections
    dma = pltpu.SemaphoreType.DMA
    f32, bf16 = jnp.float32, jnp.bfloat16
    any_spec = pl.BlockSpec(memory_space=pl.ANY)
    smem = pl.BlockSpec(memory_space=pltpu.SMEM)
    vmem = pl.BlockSpec(memory_space=pltpu.VMEM)
    out, grad = pl.pallas_call(
        functools.partial(kernel, rows, sections, plane),
        out_shape=(
            jax.ShapeDtypeStruct((sections, span, width), bf16),
            jax.ShapeDtypeStruct((rows, grain, width), f32),
        ),
        in_specs=[smem, smem, any_spec, any_spec, any_spec, any_spec],
        out_specs=(vmem, vmem),
        scratch_shapes=[
            pltpu.VMEM((blocks, slots, size, size), jnp.int32),
            pltpu.VMEM((span, width), bf16),
            pltpu.VMEM((width, width), bf16),
            pltpu.VMEM((blocks, size, slots * size), bf16),
            pltpu.VMEM((turns * blocks, size, width), bf16),
            pltpu.VMEM((sections, blocks, size), f32),
            pltpu.VMEM((count, size), f32),
            pltpu.VMEM((count, width), f32),
            pltpu.VMEM((count, width), bf16),
            pltpu.VMEM((sections, span, width), bf16),
            pltpu.VMEM((rows, grain, width), f32),
            pltpu.VMEM((rows, grain, width), bf16),
            pltpu.VMEM((rows, grain, width), bf16),
            pltpu.VMEM((sections, grain, width), f32),
            dma((4,)),
            dma((3, turns, blocks)) if plane else dma((turns, rows)),
            dma((turns, blocks)),
            dma((sections,)), dma((sections,)),
            dma((sections,)), dma((sections,)),
            dma((sections,)), dma((sections,)),
            dma((rows,)), dma((rows,)),
            dma((sections,)), dma((sections,)),
            dma((rows,)), dma((rows,)),
        ],
        compiler_params=pltpu.CompilerParams(
            collective_id=0, has_side_effects=True, vmem_limit_bytes=40 * 1024 * 1024
        ),
    )(
        live_slots, columns, features.reshape(blocks, size, width), weight,
        cotangent.reshape(sections, span, width), counts,
    )
    return out.reshape(count, width), grad.reshape(width, width)


def solution(mesh):
    rows, sections = mesh.shape["row"], mesh.shape["section"]
    in_specs = (
        P("row", None),
        P(),
        P("row", None),
        P("row", "section", None, None),
        P("row", "section"),
        P("row", "section"),
    )
    out_specs = (P("row", None), P())
    return jax.shard_map(
        functools.partial(per_device, rows, sections, (rows, sections) == (8, 4)),
        mesh=mesh, in_specs=in_specs, out_specs=out_specs, check_vma=False,
    )
```

time: 172 us -> 79.4 us (0.46)
  the two profiles are of different devices: /device:TPU:0 before, /device:TPU:31 now
where the time goes in v1:
time: 79.4 us; the launch traced here: 79.1 us
  Pallas kernels  70.9 us (89%)
  local copies, waits for them, and re-layouts  7.56 us (10%)
    pallas_call x1, Pallas kernels, per_device(): pl.pallas_call(functools.partial(kernel, rows, sections, plane), out_shap...  70.9 us
    unnamed x12, local copies, waits for them, and re-layouts  7.56 us

profile of v1, /device:TPU:31, one launch (start us, length us, event | category | flops | bytes accessed | tf_op | source)
XLA Modules:
  0.0 79.1 jit_solution(10729237377884898907)
XLA Ops:
  0.6 0.8 copy.9.cols
  1.4 0.7 copy.8.live
  2.1 0.0 copy-start
  2.1 1.6 %copy-done = s32[8,4,128,128]{3,2,1,0:T(8,128)S(1)} copy-done((s32[8,4,128,128]{3,2,1,0:T(8,128)S(1)}, s32[8,4,128,128]{3,2,1,0:T(8,128)}, u32[]{:S(2)}) %copy-start) | copy-done | bytes 2097176
  3.7 0.0 copy-start.1
  3.7 1.0 %copy-done.1 = bf16[1024,256]{1,0:T(8,128)(2,1)S(1)} copy-done((bf16[1024,256]{1,0:T(8,128)(2,1)S(1)}, bf16[1024,256]{1,0:T(8,128)(2,1)}, u32[]{:S(2)}) %copy-start.1) | copy-done | bytes 524312
  4.7 0.0 copy-start.2
  4.8 1.0 %copy-done.2 = bf16[1024,256]{1,0:T(8,128)(2,1)S(1)} copy-done((bf16[1024,256]{1,0:T(8,128)(2,1)S(1)}, bf16[1024,256]{1,0:T(8,128)(2,1)}, u32[]{:S(2)}) %copy-start.2) | copy-done | bytes 524312
  5.8 0.0 copy-start.3
  5.8 0.9 %copy-done.3 = bf16[256,256]{1,0:T(8,128)(2,1)S(1)} copy-done((bf16[256,256]{1,0:T(8,128)(2,1)S(1)}, bf16[256,256]{1,0:T(8,128)(2,1)}, u32[]{:S(2)}) %copy-start.3) | copy-done | bytes 131096
  6.7 70.9 %shard_map.77 = (bf16[4,256,256]{2,1,0:T(8,128)(2,1)S(1)}, f32[8,32,256]{2,1,0:T(8,128)S(1)}) custom-call(s32[8,1]{1,0:T(8,128)S(1)} %copy.8.live, s32[8,4]{1,0:T(8,128)S(1)} %copy.9.cols, bf16[8,128,256]{2,1,0:T(8,128)(2,1)S(1)} %bitcast.4, bf16[256,256]{1,0:T(8,128)(2,1)S(1)} %copy-done.3, bf16[4,256,256]{2,1,0:T(8,128)(2,1)S(1)} %bitcast.5, ...), custom_call_target="tpu_custom_call" | custom-call | tf_op jit(solution)/shard_map/pallas_call | solution.py:320
  77.6 0.8 %copy.12 = bf16[1024,256]{1,0:T(8,128)(2,1)} copy(bf16[1024,256]{1,0:T(8,128)(2,1)S(1)} %bitcast.6) | data formatting | bytes 1048576
  78.4 0.7 copy.13
Async XLA Ops:
  2.1 1.6 %copy-start = (s32[8,4,128,128]{3,2,1,0:T(8,128)S(1)}, s32[8,4,128,128]{3,2,1,0:T(8,128)}, u32[]{:S(2)}) copy-start(s32[8,4,128,128]{3,2,1,0:T(8,128)} %counts.1) | copy-start | bytes 6291460
  3.7 1.0 %copy-start.1 = (bf16[1024,256]{1,0:T(8,128)(2,1)S(1)}, bf16[1024,256]{1,0:T(8,128)(2,1)}, u32[]{:S(2)}) copy-start(bf16[1024,256]{1,0:T(8,128)(2,1)} %param.6) | copy-start | bytes 1572868
  4.7 1.0 %copy-start.2 = (bf16[1024,256]{1,0:T(8,128)(2,1)S(1)}, bf16[1024,256]{1,0:T(8,128)(2,1)}, u32[]{:S(2)}) copy-start(bf16[1024,256]{1,0:T(8,128)(2,1)} %param.8) | copy-start | bytes 1572868
  5.8 0.9 %copy-start.3 = (bf16[256,256]{1,0:T(8,128)(2,1)S(1)}, bf16[256,256]{1,0:T(8,128)(2,1)}, u32[]{:S(2)}) copy-start(bf16[256,256]{1,0:T(8,128)(2,1)} %weight.1) | copy-start | bytes 393220

commit v2 on v1

--- a/solution.py
+++ b/solution.py
@@ -120,7 +120,7 @@
     def prepare(b, carry):
         total = jnp.zeros((size, size), jnp.int32)
         for k in range(slots):
-            e = jnp.where(k < live[b, 0], cnt_v[b, k], 0)
+            e = jnp.where(k < live[0, b], cnt_v[b, k], 0)
             total = total + e
             edge[b, :, k * size:(k + 1) * size] = e.astype(jnp.float32).astype(jnp.bfloat16)
         d = lax.dot_general(
@@ -139,52 +139,51 @@
         deg_copies.append(d)
 
     if plane:
-        off_chip = [jnp.logical_not((y == t) & (x == home_x)) for t in range(turns)]
-        pass_on = [(y == t) & (x != home_x) for t in range(turns)]
         across = (1 - y) * 4 + x * 2 + c
+        away = x != home_x
+        far = 1 - y
+
+        @pl.when(away)
+        def _():
+            for k in range(half):
+                i = c * half + k
+                chunk(y, i, 2, sib).wait_recv()
+                chunk(y, i, 0, across).start()
+                chunk(y, i, 2, sib).start()
+
         for k in range(half):
-            for t in range(turns):
-                i = c * half + k
-
-                @pl.when(off_chip[t])
-                def _(i=i, t=t):
-                    chunk(t, i, 2, sib).wait_recv()
-                    chunk(t, i, 2, sib).start()
-
-                    @pl.when(pass_on[t])
-                    def _():
-                        chunk(t, i, 0, across).start()
+            i = c * half + k
+            chunk(far, i, 2, sib).wait_recv()
+            chunk(far, i, 2, sib).start()
+        for k in range(half):
+            chunk(far, (1 - c) * half + k, 2, sib).wait_recv()
+
+        @pl.when(away)
+        def _():
+            for k in range(half):
+                chunk(y, (1 - c) * half + k, 2, sib).wait_recv()
+
+        @pl.when((x == home_x) & (c != lax.rem(sec, 2)))
+        def _():
+            for i in range(blocks):
+                chunk(y, i, 2, sib).wait_recv()
+
         for t in range(turns):
-            def other(t=t):
-                for k in range(half):
-                    chunk(t, (1 - c) * half + k, 2, sib).wait_recv()
-
-            def mine(t=t):
-                for k in range(half):
-                    chunk(t, c * half + k, 2, sib).wait_recv()
-
-            @pl.when(jnp.logical_not(own[t]))
-            def _(other=other):
-                other()
-
-            @pl.when((y == t) & (x == home_x) & jnp.logical_not(own[t]))
-            def _(mine=mine):
-                mine()
-
             @pl.when(own[t])
             def _(t=t):
                 keep[t].wait()
 
-            def relayed(t=t):
-                for k in range(half):
-                    chunk(t, c * half + k, 2, sib).wait_send()
-
-            def crossed(t=t):
-                for k in range(half):
-                    chunk(t, c * half + k, 0, across).wait_send()
-
-            sends.append((off_chip[t], relayed))
-            sends.append((pass_on[t], crossed))
+        def crossed():
+            for k in range(half):
+                chunk(y, c * half + k, 0, across).wait_send()
+                chunk(y, c * half + k, 2, sib).wait_send()
+
+        def relayed():
+            for k in range(half):
+                chunk(far, c * half + k, 2, sib).wait_send()
+
+        sends.append((away, crossed))
+        sends.append((row >= 0, relayed))
     else:
         for t in range(turns):
             @pl.when(own[t])
@@ -200,7 +199,7 @@
         for k in range(0, slots, 2):
             picked = []
             for q in (k, k + 1):
-                g = cols[b, q]
+                g = cols[q, b]
                 picked.append(win[lax.div(lax.div(g, blocks), sections) * blocks + lax.rem(g, blocks)])
             acc = acc + jnp.dot(
                 edge[b, :, k * size:(k + 2) * size], jnp.concatenate(picked, axis=0),
@@ -263,13 +262,6 @@
         d = remote(g_send.at[peer], ga_in.at[row], ga_ssem.at[j], ga_rsem.at[row], {"row": peer})
         d.start()
         tail.append(d)
-    out_copies = []
-    for j in range(1, sections):
-        peer = lax.rem(sec + j, sections)
-        d = remote(out.at[sec], out.at[sec], o_ssem.at[j], o_rsem.at[sec], {"section": peer})
-        d.start()
-        out_copies.append(d)
-
     acc = gw32[row]
     for j in range(1, rows):
         peer = lax.rem(row + j, rows)
@@ -281,6 +273,13 @@
         d = remote(gb_in.at[sec], gb_in.at[sec], gb_ssem.at[j], gb_rsem.at[sec], {"section": peer})
         d.start()
         tail.append(d)
+    out_copies = []
+    for j in range(1, sections):
+        peer = lax.rem(sec + j, sections)
+        d = remote(out.at[sec], out.at[sec], o_ssem.at[j], o_rsem.at[sec], {"section": peer})
+        d.start()
+        out_copies.append(d)
+
     for j in range(1, sections):
         peer = lax.rem(sec + j, sections)
         remote(gb_in.at[peer], gb_in.at[peer], gb_ssem.at[j], gb_rsem.at[peer], {"section": peer}).wait_recv()
@@ -314,7 +313,7 @@
     turns = rows // sections
     dma = pltpu.SemaphoreType.DMA
     f32, bf16 = jnp.float32, jnp.bfloat16
-    any_spec = pl.BlockSpec(memory_space=pl.ANY)
+    any_spec = pl.BlockSpec(memory_space=pltpu.HBM)
     smem = pl.BlockSpec(memory_space=pltpu.SMEM)
     vmem = pl.BlockSpec(memory_space=pltpu.VMEM)
     out, grad = pl.pallas_call(
@@ -351,10 +350,10 @@
             dma((rows,)), dma((rows,)),
         ],
         compiler_params=pltpu.CompilerParams(
-            collective_id=0, has_side_effects=True, vmem_limit_bytes=40 * 1024 * 1024
+            collective_id=0, has_side_effects=True, vmem_limit_bytes=62 * 1024 * 1024
         ),
     )(
-        live_slots, columns, features.reshape(blocks, size, width), weight,
+        live_slots.T, columns.T, features.reshape(blocks, size, width), weight,
         cotangent.reshape(sections, span, width), counts,
     )
     return out.reshape(count, width), grad.reshape(width, width)

time: 79.4 us -> 54.4 us (0.69)
  the two profiles are of different devices: /device:TPU:31 before, /device:TPU:27 now
where the time goes in v2:
time: 54.4 us; the launch traced here: 54.2 us
  Pallas kernels  50 us (92%)
  local copies, waits for them, and re-layouts  3.54 us (7%)
  between operations  0.64 us (1%)
    pallas_call x1, Pallas kernels, per_device(): pl.pallas_call(functools.partial(kernel, rows, sections, plane), out_shap...  50 us
    unnamed x2, local copies, waits for them, and re-layouts  3.54 us

profile of v2, /device:TPU:27, one launch (start us, length us, event | category | flops | bytes accessed | tf_op | source)
XLA Modules:
  0.0 54.2 jit_solution(18094654764447749423)
XLA Ops:
  0.6 50.0 %shard_map.77 = (bf16[4,256,256]{2,1,0:T(8,128)(2,1)}, f32[8,32,256]{2,1,0:T(8,128)}) custom-call(s32[1,8]{1,0:T(1,128)} %bitcast.11, s32[4,8]{1,0:T(4,128)} %bitcast.10, bf16[8,128,256]{2,1,0:T(8,128)(2,1)} %bitcast.6, bf16[256,256]{1,0:T(8,128)(2,1)} %weight.1, bf16[4,256,256]{2,1,0:T(8,128)(2,1)} %bitcast.7, s32[8,4,128,128]{3,2,1,0:T(8,128)} %counts.1), custom_call_target="tpu_custom_call" | custom-call | tf_op jit(solution)/shard_map/pallas_call | solution.py:319
  50.7 1.9 %copy.10 = bf16[1024,256]{1,0:T(8,128)(2,1)} copy(bf16[1024,256]{1,0:T(8,128)(2,1)} %bitcast.8) | data formatting | bytes 1048576
  52.5 1.7 %copy.11 = f32[256,256]{1,0:T(8,128)} copy(f32[256,256]{1,0:T(8,128)} %bitcast.9) | data formatting | bytes 524288

commit v3 on v2

--- a/solution.py
+++ b/solution.py
@@ -22,7 +22,7 @@
     live, cols, feat, weight, cot, counts,
     out, gw_out,
     cnt_v, cot_v, w_v, edge, win, deg_all, scale, part32, part16, rs_in,
-    gw32, g_send, ga_in, gb_in,
+    gw32, ga_in, gb_in,
     l_sem, f_ssem, f_rsem, d_ssem, d_rsem, rs_ssem, rs_rsem, o_ssem, o_rsem,
     ga_ssem, ga_rsem, gb_ssem, gb_rsem, gc_ssem, gc_rsem,
 ):
@@ -254,38 +254,52 @@
     grad = lax.dot_general(aggregate, grad_pre, (((0,), (0,)), ((), ())), preferred_element_type=jnp.float32)
     grad = grad.reshape(rows, grain, width)
     gw32[...] = grad
-    g_send[...] = grad.astype(jnp.bfloat16)
+
+    out_copies = []
+    if plane:
+        inner = (sec == 1) | (sec == 2)
+        mate = sec + 1 - 2 * lax.rem(sec, 2)
+        other_side = 2 - 2 * (sec // 2)
+        targets = [2 - sec // 2, mate]
+    else:
+        targets = [lax.rem(sec + j, sections) for j in range(1, sections)]
+    for j, peer in enumerate(targets):
+        d = remote(out.at[sec], out.at[sec], o_ssem.at[j], o_rsem.at[sec], {"section": peer})
+        d.start()
+        out_copies.append(d)
 
     tail = []
     for j in range(1, rows):
         peer = lax.rem(row + j, rows)
-        d = remote(g_send.at[peer], ga_in.at[row], ga_ssem.at[j], ga_rsem.at[row], {"row": peer})
+        d = remote(gw32.at[peer], ga_in.at[row], ga_ssem.at[j], ga_rsem.at[row], {"row": peer})
         d.start()
         tail.append(d)
     acc = gw32[row]
     for j in range(1, rows):
         peer = lax.rem(row + j, rows)
         remote(ga_in.at[peer], ga_in.at[peer], ga_ssem.at[j], ga_rsem.at[peer], {"row": peer}).wait_recv()
-        acc = acc + ga_in[peer].astype(jnp.float32)
-    gb_in[sec] = acc
+        acc = acc + ga_in[peer]
+    gb_in[sec] = acc.astype(jnp.bfloat16)
     for j in range(1, sections):
         peer = lax.rem(sec + j, sections)
         d = remote(gb_in.at[sec], gb_in.at[sec], gb_ssem.at[j], gb_rsem.at[sec], {"section": peer})
         d.start()
         tail.append(d)
-    out_copies = []
-    for j in range(1, sections):
-        peer = lax.rem(sec + j, sections)
-        d = remote(out.at[sec], out.at[sec], o_ssem.at[j], o_rsem.at[sec], {"section": peer})
-        d.start()
-        out_copies.append(d)
+    if plane:
+        @pl.when(inner)
+        def _():
+            for q in range(2):
+                at = other_side + q
+                carry = remote(out.at[at], out.at[at], o_ssem.at[2 + q], o_rsem.at[at], {"section": mate})
+                carry.wait_recv()
+                carry.start()
 
     for j in range(1, sections):
         peer = lax.rem(sec + j, sections)
         remote(gb_in.at[peer], gb_in.at[peer], gb_ssem.at[j], gb_rsem.at[peer], {"section": peer}).wait_recv()
-    acc = gb_in[0]
+    acc = gb_in[0].astype(jnp.float32)
     for z in range(1, sections):
-        acc = acc + gb_in[z]
+        acc = acc + gb_in[z].astype(jnp.float32)
     gw_out[row] = acc
     for j in range(1, rows):
         peer = lax.rem(row + j, rows)
@@ -295,9 +309,25 @@
     for j in range(1, rows):
         peer = lax.rem(row + j, rows)
         remote(gw_out.at[peer], gw_out.at[peer], gc_ssem.at[j], gc_rsem.at[peer], {"row": peer}).wait_recv()
-    for j in range(1, sections):
-        peer = lax.rem(sec + j, sections)
-        remote(out.at[peer], out.at[peer], o_ssem.at[j], o_rsem.at[peer], {"section": peer}).wait_recv()
+    def landed(at):
+        remote(out.at[at], out.at[at], o_ssem.at[0], o_rsem.at[at], {"section": lax.rem(sec + 1, sections)}).wait_recv()
+
+    if plane:
+        landed(mate)
+
+        @pl.when(jnp.logical_not(inner))
+        def _():
+            for q in range(2):
+                landed(other_side + q)
+
+        @pl.when(inner)
+        def _():
+            for q in range(2):
+                at = other_side + q
+                remote(out.at[at], out.at[at], o_ssem.at[2 + q], o_rsem.at[at], {"section": mate}).wait_send()
+    else:
+        for j in range(1, sections):
+            landed(lax.rem(sec + j, sections))
 
     for cond, finish in sends:
         pl.when(cond)(finish)
@@ -336,9 +366,8 @@
             pltpu.VMEM((count, width), bf16),
             pltpu.VMEM((sections, span, width), bf16),
             pltpu.VMEM((rows, grain, width), f32),
-            pltpu.VMEM((rows, grain, width), bf16),
-            pltpu.VMEM((rows, grain, width), bf16),
-            pltpu.VMEM((sections, grain, width), f32),
+            pltpu.VMEM((rows, grain, width), f32),
+            pltpu.VMEM((sections, grain, width), bf16),
             dma((4,)),
             dma((3, turns, blocks)) if plane else dma((turns, rows)),
             dma((turns, blocks)),

time: 54.4 us -> 53.9 us (level)
  the two profiles are of different devices: /device:TPU:27 before, /device:TPU:0 now
where the time goes in v3:
time: 53.9 us; the launch traced here: 53.7 us
  Pallas kernels  49.5 us (92%)
  local copies, waits for them, and re-layouts  3.54 us (7%)
  between operations  0.64 us (1%)
    pallas_call x1, Pallas kernels, per_device(): pl.pallas_call(functools.partial(kernel, rows, sections, plane), out_shap...  49.5 us
    unnamed x2, local copies, waits for them, and re-layouts  3.54 us

profile of v3, /device:TPU:0, one launch (start us, length us, event | category | flops | bytes accessed | tf_op | source)
XLA Modules:
  0.0 53.7 jit_solution(18062457182831053197)
XLA Ops:
  0.6 49.5 %shard_map.77 = (bf16[4,256,256]{2,1,0:T(8,128)(2,1)}, f32[8,32,256]{2,1,0:T(8,128)}) custom-call(s32[1,8]{1,0:T(1,128)} %bitcast.11, s32[4,8]{1,0:T(4,128)} %bitcast.10, bf16[8,128,256]{2,1,0:T(8,128)(2,1)} %bitcast.6, bf16[256,256]{1,0:T(8,128)(2,1)} %weight.1, bf16[4,256,256]{2,1,0:T(8,128)(2,1)} %bitcast.7, s32[8,4,128,128]{3,2,1,0:T(8,128)} %counts.1), custom_call_target="tpu_custom_call" | custom-call | tf_op jit(solution)/shard_map/pallas_call | solution.py:349
  50.2 1.9 %copy.10 = bf16[1024,256]{1,0:T(8,128)(2,1)} copy(bf16[1024,256]{1,0:T(8,128)(2,1)} %bitcast.8) | data formatting | bytes 1048576
  52.0 1.7 %copy.11 = f32[256,256]{1,0:T(8,128)} copy(f32[256,256]{1,0:T(8,128)} %bitcast.9) | data formatting | bytes 524288

commit v4 on v3

--- a/solution.py
+++ b/solution.py
@@ -343,6 +343,7 @@
     turns = rows // sections
     dma = pltpu.SemaphoreType.DMA
     f32, bf16 = jnp.float32, jnp.bfloat16
+    pin = lambda a: pltpu.with_memory_space_constraint(a, pltpu.HBM)
     any_spec = pl.BlockSpec(memory_space=pltpu.HBM)
     smem = pl.BlockSpec(memory_space=pltpu.SMEM)
     vmem = pl.BlockSpec(memory_space=pltpu.VMEM)
@@ -379,11 +380,11 @@
             dma((rows,)), dma((rows,)),
         ],
         compiler_params=pltpu.CompilerParams(
-            collective_id=0, has_side_effects=True, vmem_limit_bytes=62 * 1024 * 1024
+            collective_id=0, has_side_effects=True, vmem_limit_bytes=40 * 1024 * 1024
         ),
     )(
-        live_slots.T, columns.T, features.reshape(blocks, size, width), weight,
-        cotangent.reshape(sections, span, width), counts,
+        pin(live_slots.T), pin(columns.T), pin(features.reshape(blocks, size, width)), pin(weight),
+        pin(cotangent.reshape(sections, span, width)), pin(counts),
     )
     return out.reshape(count, width), grad.reshape(width, width)
 

time: 53.9 us -> 50.9 us (0.944)
  local copies, waits for them, and re-layouts: 3.54 us -> 1.5 us
  Pallas kernels: 49.5 us -> 48.6 us
    unnamed x2, local copies, waits for them, and re-layouts: 3.54 us -> 1.5 us
    pallas_call x1, Pallas kernels: 49.5 us -> 48.6 us  [per_device(): pl.pallas_call(functools.partial(kernel, rows, sections, plane), out_shap...]
where the time goes in v4:
time: 50.9 us; the launch traced here: 50.8 us
  Pallas kernels  48.6 us (95%)
  local copies, waits for them, and re-layouts  1.5 us (3%)
  between operations  0.64 us (1%)
    pallas_call x1, Pallas kernels, per_device(): pl.pallas_call(functools.partial(kernel, rows, sections, plane), out_shap...  48.6 us
    unnamed x2, local copies, waits for them, and re-layouts  1.5 us

profile of v4, /device:TPU:0, one launch (start us, length us, event | category | flops | bytes accessed | tf_op | source)
XLA Modules:
  0.0 50.8 jit_solution(705382925687057505)
XLA Ops:
  0.6 48.6 %shard_map.77 = (bf16[4,256,256]{2,1,0:T(8,128)(2,1)S(1)}, f32[8,32,256]{2,1,0:T(8,128)S(1)}) custom-call(s32[1,8]{1,0:T(1,128)} %bitcast.11, s32[4,8]{1,0:T(4,128)} %bitcast.10, bf16[8,128,256]{2,1,0:T(8,128)(2,1)} %bitcast.8, bf16[256,256]{1,0:T(8,128)(2,1)} %weight.1, bf16[4,256,256]{2,1,0:T(8,128)(2,1)} %bitcast.9, s32[8,4,128,128]{3,2,1,0:T(8,128)} %counts.1), custom_call_target="tpu_custom_call" | custom-call | tf_op jit(solution)/shard_map/pallas_call | solution.py:350
  49.3 0.8 %copy.10 = bf16[1024,256]{1,0:T(8,128)(2,1)} copy(bf16[1024,256]{1,0:T(8,128)(2,1)S(1)} %bitcast.6) | data formatting | bytes 1048576
  50.1 0.7 %copy.11 = f32[256,256]{1,0:T(8,128)} copy(f32[256,256]{1,0:T(8,128)S(1)} %bitcast.7) | data formatting | bytes 524288

commit v5 on v4

--- a/solution.py
+++ b/solution.py
@@ -214,8 +214,10 @@
         for b in range(blocks):
             block_sum(b)
     rs_copies = []
-    for j in range(1, sections + 1):
-        peer = lax.rem(sec + j, sections)
+    order = [lax.rem(sec + j, sections) for j in range(1, sections + 1)]
+    if plane:
+        order = [sec + 2 - 4 * (sec // 2), 3 - sec, sec + 1 - 2 * lax.rem(sec, 2), sec]
+    for j, peer in enumerate(order, 1):
         for q in range(per):
             block_sum(peer * per + q)
         if j < sections:

time: 50.9 us -> 50.2 us (0.986)
  Pallas kernels: 48.6 us -> 47.9 us
    pallas_call x1, Pallas kernels: 48.6 us -> 47.9 us  [per_device(): pl.pallas_call(functools.partial(kernel, rows, sections, plane), out_shap...]
where the time goes in v5:
time: 50.2 us; the launch traced here: 50 us
  Pallas kernels  47.9 us (95%)
  local copies, waits for them, and re-layouts  1.5 us (3%)
  between operations  0.64 us (1%)
    pallas_call x1, Pallas kernels, per_device(): pl.pallas_call(functools.partial(kernel, rows, sections, plane), out_shap...  47.9 us
    unnamed x2, local copies, waits for them, and re-layouts  1.5 us

profile of v5, /device:TPU:0, one launch (start us, length us, event | category | flops | bytes accessed | tf_op | source)
XLA Modules:
  0.0 50.0 jit_solution(3305601646133318019)
XLA Ops:
  0.6 47.9 %shard_map.77 = (bf16[4,256,256]{2,1,0:T(8,128)(2,1)S(1)}, f32[8,32,256]{2,1,0:T(8,128)S(1)}) custom-call(s32[1,8]{1,0:T(1,128)} %bitcast.11, s32[4,8]{1,0:T(4,128)} %bitcast.10, bf16[8,128,256]{2,1,0:T(8,128)(2,1)} %bitcast.8, bf16[256,256]{1,0:T(8,128)(2,1)} %weight.1, bf16[4,256,256]{2,1,0:T(8,128)(2,1)} %bitcast.9, s32[8,4,128,128]{3,2,1,0:T(8,128)} %counts.1), custom_call_target="tpu_custom_call" | custom-call | tf_op jit(solution)/shard_map/pallas_call | solution.py:352
  48.5 0.8 %copy.10 = bf16[1024,256]{1,0:T(8,128)(2,1)} copy(bf16[1024,256]{1,0:T(8,128)(2,1)S(1)} %bitcast.6) | data formatting | bytes 1048576
  49.3 0.7 %copy.11 = f32[256,256]{1,0:T(8,128)} copy(f32[256,256]{1,0:T(8,128)S(1)} %bitcast.7) | data formatting | bytes 524288
